TPU v7x, 256 devices: a whole 4x4x8 slice. The times are simulated.
256 devices in a mesh: seq: 32 (over z, x), heads: 8 (over y, core).
Axes of the slice: x: 4, y: 4, z: 8, core: 2. Of those that a mesh axis runs over, the one named last changes fastest.
Arguments:
- lin_q: bfloat16 [8192, 8192], P('seq', 'heads'), may hold values from -4 to 4
- lin_k: bfloat16 [8192, 8192], P('seq', 'heads'), may hold values from -4 to 4
- lin_v: bfloat16 [8192, 8192], P('seq', 'heads'), may hold values from -6 to 6
- decay_rates: float32 [64], P('heads'), may hold values from 3.0517578e-05 to 0.03125
- norm_gain: float32 [8192], P('heads'), may hold values from 0.25 to 1.75
- soft_q: bfloat16 [8192, 8192], P('seq', 'heads'), may hold values from -8 to 8
- soft_k: bfloat16 [8192, 1024], P('seq', 'heads'), may hold values from -8 to 8
- soft_v: bfloat16 [8192, 1024], P('seq', 'heads'), may hold values from -6 to 6
- segment_ids: int32 [8192], P('seq'), may hold values from 0 to 3, never falling along the last dimension, each value on 1 to 6144 neighbouring positions
Outputs:
- lin_out: bfloat16 [8192, 8192], P('seq', 'heads')
- soft_out: bfloat16 [8192, 8192], P('seq', 'heads')
Inputs may be any that keep to these rules, and one draw needn't show every extreme that they name: `segment_ids`: never falling along the sequence; each document has 1 to 6144 tokens, one exactly that many.
All inputs are finite; a program needn't handle non-finite values.
Results may differ from a plain program's by a relative error of at most 0.0049.
Values may be sent and summed in bfloat16 or wider, within the bound.
A program may use at most 128 MiB of HBM per device.

v0:
```python
from functools import partial
import math
import jax
import jax.numpy as jnp
from jax import lax
from jax.sharding import PartitionSpec as P

BLOCK = 256


def carried_in(part, axis, combine, identity):
    place = lax.axis_index(axis)
    gathered = jax.tree.map(lambda a: lax.all_gather(a, axis), part)
    state = jax.tree.map(lambda a, e: jnp.zeros_like(a) + jnp.asarray(e, a.dtype), part, identity)

    def carried_one(step, state):
        return combine(
            state, jax.tree.map(lambda a: lax.dynamic_index_in_dim(a, step, 0, False), gathered)
        )

    return lax.fori_loop(0, place, carried_one, state)


def light_block(carry, inputs, rates):
    state, last_prev = carry
    q_blk, k_blk, v_blk, seg_blk = inputs
    size = q_blk.shape[0]
    seg_f = seg_blk.astype(jnp.float32)
    pos = jnp.arange(size).astype(jnp.float32)
    diff = pos[:, None] - pos[None, :]
    linked = (diff >= 0.0) & (seg_f[:, None] == seg_f[None, :])
    decay = jnp.exp(-rates[:, None, None] * jnp.maximum(diff, 0.0)[None])
    scores = jnp.einsum("thd,shd->hts", q_blk, k_blk, preferred_element_type=jnp.float32)
    weights = jnp.where(linked[None], scores * decay, 0.0).astype(jnp.bfloat16)
    intra = jnp.einsum("hts,shd->thd", weights, v_blk, preferred_element_type=jnp.float32)
    use = (seg_f == last_prev).astype(jnp.float32)
    coef = jnp.exp(-rates[None, :] * (pos[:, None] + 1.0)) * use[:, None]
    q_state = jnp.einsum(
        "thd,hde->the", q_blk.astype(jnp.float32), state, precision=lax.Precision.HIGHEST
    )
    out = intra + coef[:, :, None] * q_state
    last = seg_f[-1]
    k_weight = (
        jnp.exp(-rates[None, :] * (size - 1.0 - pos[:, None]))
        * (seg_f == last).astype(jnp.float32)[:, None]
    )
    k_dec = (k_blk.astype(jnp.float32) * k_weight[:, :, None]).astype(jnp.bfloat16)
    local = jnp.einsum("shd,she->hde", k_dec, v_blk, preferred_element_type=jnp.float32)
    keep = jnp.where(last == last_prev, 1.0, 0.0) * jnp.exp(-rates * size)
    return ((keep[:, None, None] * state + local, last), out)


def combine_states(earlier, later):
    state_e, dec_e, last_e = earlier
    state_l, dec_l, last_l = later
    match = (last_e == last_l) | (last_l < 0.0)
    factor = jnp.where(match, dec_l, 0.0)
    return (factor[:, None, None] * state_e + state_l, dec_e * dec_l, jnp.maximum(last_e, last_l))


def block_update(inner, queries, qpos, seg_rows, k_blk, v_blk, s_blk, kpos, scale):
    mx, den, acc = inner
    shared_heads = k_blk.shape[1]
    group = queries.shape[2]
    query_count = queries.shape[0]
    key_count = k_blk.shape[0]
    heads = shared_heads * group
    s = (
        jnp.einsum("tgjd,sgd->gjts", queries, k_blk, preferred_element_type=jnp.float32).reshape(
            heads, query_count, key_count
        )
        * scale
    )
    mask = (kpos[None, :] <= qpos[:, None]) & (s_blk[None, :] == seg_rows[:, None])
    top = jnp.max(jnp.where(mask[None], s, -1e30), axis=2)
    new_mx = jnp.maximum(mx, top)
    corr = jnp.exp(mx - new_mx)
    p = jnp.where(mask[None], jnp.exp(s - new_mx[:, :, None]), 0.0)
    den = den * corr + jnp.sum(p, axis=2)
    weights = p.astype(jnp.bfloat16).reshape(shared_heads, group, query_count, key_count)
    mixed = jnp.einsum(
        "gjts,sgd->gjtd", weights, v_blk, preferred_element_type=jnp.float32
    ).reshape(heads, query_count, -1)
    acc = acc * corr[:, :, None] + mixed
    return (new_mx, den, acc)


def body(lin_q, lin_k, lin_v, decay_rates, norm_gain, soft_q, soft_k, soft_v, segment_ids):
    tok = lin_q.shape[0]
    heads = decay_rates.shape[0]
    width = lin_q.shape[1] // heads
    blocks = tok // BLOCK
    shape4 = (blocks, BLOCK, heads, width)
    init = (jnp.zeros((heads, width, width), jnp.float32), jnp.float32(-1.0))
    step_fn = lambda c, x: light_block(c, x, decay_rates)
    (state_loc, last_loc), outs = lax.scan(
        step_fn,
        init,
        (
            lin_q.reshape(shape4),
            lin_k.reshape(shape4),
            lin_v.reshape(shape4),
            segment_ids.reshape(blocks, BLOCK),
        ),
    )
    local_out = outs.reshape(tok, heads, width)
    summary = (state_loc, jnp.exp(-decay_rates * tok), last_loc.reshape(1))
    identity = (
        jnp.zeros((heads, width, width), jnp.float32),
        jnp.ones((heads,), jnp.float32),
        jnp.full((1,), -1.0, jnp.float32),
    )
    state_in, dec_in, last_in = carried_in(summary, "seq", combine_states, identity)
    seg_f = segment_ids.astype(jnp.float32)
    pos = jnp.arange(tok).astype(jnp.float32)
    coef = (
        jnp.exp(-decay_rates[None, :] * (pos[:, None] + 1.0))
        * (seg_f == last_in[0]).astype(jnp.float32)[:, None]
    )
    q_three = lin_q.reshape(tok, heads, width)
    q_state = jnp.einsum(
        "thd,hde->the", q_three.astype(jnp.float32), state_in, precision=lax.Precision.HIGHEST
    )
    raw = (local_out + coef[:, :, None] * q_state).reshape(tok, heads * width)
    sums = jnp.sum(raw * raw, axis=1)
    total_sq = lax.psum(sums, "heads")
    count = lax.axis_size("heads") * heads * width
    lin_out = (raw * lax.rsqrt(total_sq / count + 1e-06)[:, None] * norm_gain[None, :]).astype(
        jnp.bfloat16
    )
    scale = 1.0 / math.sqrt(width)
    shared_heads = soft_k.shape[1] // width
    group = heads // shared_heads
    mine = lax.axis_index("seq")
    plans = (soft_q, segment_ids, mine * tok)
    query_sets = []
    query_rows, seg_rows, first = plans
    count_rows = query_rows.shape[0]
    query_sets.append(
        (
            query_rows.reshape(count_rows, shared_heads, group, width),
            first + jnp.arange(count_rows),
            seg_rows,
            first + count_rows - 1,
        )
    )
    start_carry = tuple(
        (
            (
                jnp.full((heads, qs[0].shape[0]), -1e30, jnp.float32),
                jnp.zeros((heads, qs[0].shape[0]), jnp.float32),
                jnp.zeros((heads, qs[0].shape[0], width), jnp.float32),
            )
            for qs in query_sets
        )
    )
    carry = start_carry
    keys = lax.all_gather(soft_k, "seq", axis=0, tiled=True)
    values = lax.all_gather(soft_v, "seq", axis=0, tiled=True)
    seg_keys = lax.all_gather(segment_ids, "seq", axis=0, tiled=True)
    length = keys.shape[0]
    rows = math.gcd(length, 1024)
    count_blk = length // rows
    k_blocks = keys.reshape(count_blk, rows, shared_heads, width)
    v_blocks = values.reshape(count_blk, rows, shared_heads, width)
    s_blocks = seg_keys.reshape(count_blk, rows)

    def attend_one(state, item):
        k_blk, v_blk, s_blk, index = item
        blk_start = index * rows
        kpos = blk_start + jnp.arange(rows)
        fresh = []
        for query_set, inner in zip(query_sets, state):
            queries, qpos, seg_rows, last_pos = query_set
            update = partial(
                block_update,
                queries=queries,
                qpos=qpos,
                seg_rows=seg_rows,
                k_blk=k_blk,
                v_blk=v_blk,
                s_blk=s_blk,
                kpos=kpos,
                scale=scale,
            )
            inner = update(inner)
            fresh.append(inner)
        return (tuple(fresh), None)

    carry, _ = lax.scan(attend_one, carry, (k_blocks, v_blocks, s_blocks, jnp.arange(count_blk)))
    outputs = []
    for mx, den, acc in carry:
        outputs.append(
            (acc / den[:, :, None])
            .transpose(1, 0, 2)
            .reshape(acc.shape[1], heads * width)
            .astype(jnp.bfloat16)
        )
    soft_out = outputs[0]
    return (lin_out, soft_out)


def solution(mesh):
    placed = (
        P("seq", "heads"),
        P("seq", "heads"),
        P("seq", "heads"),
        P("heads"),
        P("heads"),
        P("seq", "heads"),
        P("seq", "heads"),
        P("seq", "heads"),
        P("seq"),
    )
    return jax.shard_map(
        body,
        mesh=mesh,
        in_specs=placed,
        out_specs=(P("seq", "heads"), P("seq", "heads")),
        check_vma=False,
    )
```

profile of v0, /device:TPU:230, one launch (start us, length us, event | category | flops | bytes accessed | tf_op | source)
XLA Modules:
  0.0 448.4 jit_solution(15058796765951390284)
XLA Ops:
  9.4 1.2 copy.50
  10.7 1.3 dynamic-slice.1
  12.6 1.2 fusion.61
  14.5 1.3 compare_convert_fusion.1
  16.6 2.1 convolution_add_fusion
  18.8 69.7 %all-reduce.2 = (f32[32]{0:T(128)S(1)}, f32[256]{0:T(256)S(1)}) all-reduce(f32[32]{0:T(128)S(1)} %get-tuple-element.258, f32[256]{0:T(256)S(1)} %get-tuple-element.260), channel_id=2, replica_groups=mesh['seq'=32,'heads'=8] {'seq'}, use_global_device_ids=true, to_apply=%add | all-reduce | flops 288 | bytes 2304
  88.6 1.3 copy.44
  90.2 43.2 %all-gather.3 = s32[32,1,256]{2,1,0:T(1,128)S(1)} all-gather(s32[1,1,256]{2,1,0:T(1,128)} %bitcast.157), channel_id=1, replica_groups=mesh['seq'=32,'heads'=8] {'seq'}, dimensions={0}, use_global_device_ids=true | all-gather | bytes 33792 | tf_op jit(solution)/shard_map/all_gather | solution.py:160
  133.8 29.7 %all-gather.10.cloned.1.call-done = bf16[8192,128]{1,0:T(8,128)(2,1)} async-done(((bf16[256,128]{1,0:T(8,128)(2,1)}), bf16[8192,128]{1,0:T(8,128)(2,1)}) %all-gather.10.cloned.1.call-update) | async-done | bytes 2097168 | tf_op jit(solution)/shard_map/all_gather | solution.py:159
  163.5 139.9 %while.36 = (s32[]{:T(128)}, f32[8,256]{1,0:T(8,128)S(1)}, f32[8,256]{1,0:T(8,128)S(1)}, f32[8,256,128]{2,1,0:T(8,128)S(1)}, s32[8]{0:T(128)S(1)}, /*index=5*/s3...) while((s32[]{:T(128)}, f32[8,256]{1,0:T(8,128)S(1)}, ...), condition=%wide.region_7.8_spmd.clone, body=%wide.region_4.7_spmd.clone.sunk | while | flops 1098394880 | bytes 63070416 | solution.py:190
  165.9 5.6 %fusion.80 = (f32[8,256]{1,0:T(8,128)S(1)}, f32[1024,256,8]{1,0,2:T(8,128)}) fusion(pred[256,1024]{0,1:T(8,128)(4,1)S(1)} %compare_and_fusion.2, bf16[256,1,8,128]{3,0,2,1:T(8,128)(2,1)S(1)} %get-tuple-element.452, bf16[8,1024,1,128]{3,1,2,0:T(8,128)(2,1)} %get-tuple-element.451, s32[]{:T(128)} %get-tuple-element.430), kind=kOutput, calls=%fused_computation.8.clone.1 | convolution fusion | flops 543160320 | bytes 9445888 | tf_op jit(solution)/shard_map/while/body/eval_jaxpr/tgjd,sgd->gjts/dot_general | solution.py:69
  171.5 5.2 %fusion.81 = f32[8,256]{1,0:T(8,128)S(1)} fusion(f32[1024,256,8]{1,0,2:T(8,128)} %get-tuple-element.380, f32[8,256]{1,0:T(8,128)S(1)} %select_maximum_fusion.2, pred[256,1024]{0,1:T(8,128)(4,1)S(1)} %compare_and_fusion.2), kind=kLoop, calls=%fused_computation.11.clone.1 | loop fusion | flops 8386560 | bytes 8667136 | tf_op jit(solution)/shard_map/while/body/eval_jaxpr/reduce_sum | solution.py:79
  177.3 3.4 fusion.83
  183.2 5.6 %fusion.80 = (f32[8,256]{1,0:T(8,128)S(1)}, f32[1024,256,8]{1,0,2:T(8,128)}) fusion(pred[256,1024]{0,1:T(8,128)(4,1)S(1)} %compare_and_fusion.2, bf16[256,1,8,128]{3,0,2,1:T(8,128)(2,1)S(1)} %get-tuple-element.452, bf16[8,1024,1,128]{3,1,2,0:T(8,128)(2,1)} %get-tuple-element.451, s32[]{:T(128)} %get-tuple-element.430), kind=kOutput, calls=%fused_computation.8.clone.1 | convolution fusion | flops 543160320 | bytes 9445888 | tf_op jit(solution)/shard_map/while/body/eval_jaxpr/tgjd,sgd->gjts/dot_general | solution.py:69
  188.8 5.3 %fusion.81 = f32[8,256]{1,0:T(8,128)S(1)} fusion(f32[1024,256,8]{1,0,2:T(8,128)} %get-tuple-element.380, f32[8,256]{1,0:T(8,128)S(1)} %select_maximum_fusion.2, pred[256,1024]{0,1:T(8,128)(4,1)S(1)} %compare_and_fusion.2), kind=kLoop, calls=%fused_computation.11.clone.1 | loop fusion | flops 8386560 | bytes 8667136 | tf_op jit(solution)/shard_map/while/body/eval_jaxpr/reduce_sum | solution.py:79
  194.8 3.4 fusion.83
  200.7 5.6 %fusion.80 = (f32[8,256]{1,0:T(8,128)S(1)}, f32[1024,256,8]{1,0,2:T(8,128)}) fusion(pred[256,1024]{0,1:T(8,128)(4,1)S(1)} %compare_and_fusion.2, bf16[256,1,8,128]{3,0,2,1:T(8,128)(2,1)S(1)} %get-tuple-element.452, bf16[8,1024,1,128]{3,1,2,0:T(8,128)(2,1)} %get-tuple-element.451, s32[]{:T(128)} %get-tuple-element.430), kind=kOutput, calls=%fused_computation.8.clone.1 | convolution fusion | flops 543160320 | bytes 9445888 | tf_op jit(solution)/shard_map/while/body/eval_jaxpr/tgjd,sgd->gjts/dot_general | solution.py:69
  206.3 5.2 %fusion.81 = f32[8,256]{1,0:T(8,128)S(1)} fusion(f32[1024,256,8]{1,0,2:T(8,128)} %get-tuple-element.380, f32[8,256]{1,0:T(8,128)S(1)} %select_maximum_fusion.2, pred[256,1024]{0,1:T(8,128)(4,1)S(1)} %compare_and_fusion.2), kind=kLoop, calls=%fused_computation.11.clone.1 | loop fusion | flops 8386560 | bytes 8667136 | tf_op jit(solution)/shard_map/while/body/eval_jaxpr/reduce_sum | solution.py:79
  212.1 3.4 fusion.83
  218.0 6.0 %fusion.80 = (f32[8,256]{1,0:T(8,128)S(1)}, f32[1024,256,8]{1,0,2:T(8,128)}) fusion(pred[256,1024]{0,1:T(8,128)(4,1)S(1)} %compare_and_fusion.2, bf16[256,1,8,128]{3,0,2,1:T(8,128)(2,1)S(1)} %get-tuple-element.452, bf16[8,1024,1,128]{3,1,2,0:T(8,128)(2,1)} %get-tuple-element.451, s32[]{:T(128)} %get-tuple-element.430), kind=kOutput, calls=%fused_computation.8.clone.1 | convolution fusion | flops 543160320 | bytes 9445888 | tf_op jit(solution)/shard_map/while/body/eval_jaxpr/tgjd,sgd->gjts/dot_general | solution.py:69
  223.9 5.3 %fusion.81 = f32[8,256]{1,0:T(8,128)S(1)} fusion(f32[1024,256,8]{1,0,2:T(8,128)} %get-tuple-element.380, f32[8,256]{1,0:T(8,128)S(1)} %select_maximum_fusion.2, pred[256,1024]{0,1:T(8,128)(4,1)S(1)} %compare_and_fusion.2), kind=kLoop, calls=%fused_computation.11.clone.1 | loop fusion | flops 8386560 | bytes 8667136 | tf_op jit(solution)/shard_map/while/body/eval_jaxpr/reduce_sum | solution.py:79
  229.9 3.5 fusion.83
  235.8 5.6 %fusion.80 = (f32[8,256]{1,0:T(8,128)S(1)}, f32[1024,256,8]{1,0,2:T(8,128)}) fusion(pred[256,1024]{0,1:T(8,128)(4,1)S(1)} %compare_and_fusion.2, bf16[256,1,8,128]{3,0,2,1:T(8,128)(2,1)S(1)} %get-tuple-element.452, bf16[8,1024,1,128]{3,1,2,0:T(8,128)(2,1)} %get-tuple-element.451, s32[]{:T(128)} %get-tuple-element.430), kind=kOutput, calls=%fused_computation.8.clone.1 | convolution fusion | flops 543160320 | bytes 9445888 | tf_op jit(solution)/shard_map/while/body/eval_jaxpr/tgjd,sgd->gjts/dot_general | solution.py:69
  241.4 5.3 %fusion.81 = f32[8,256]{1,0:T(8,128)S(1)} fusion(f32[1024,256,8]{1,0,2:T(8,128)} %get-tuple-element.380, f32[8,256]{1,0:T(8,128)S(1)} %select_maximum_fusion.2, pred[256,1024]{0,1:T(8,128)(4,1)S(1)} %compare_and_fusion.2), kind=kLoop, calls=%fused_computation.11.clone.1 | loop fusion | flops 8386560 | bytes 8667136 | tf_op jit(solution)/shard_map/while/body/eval_jaxpr/reduce_sum | solution.py:79
  247.7 3.4 fusion.83
  253.6 5.6 %fusion.80 = (f32[8,256]{1,0:T(8,128)S(1)}, f32[1024,256,8]{1,0,2:T(8,128)}) fusion(pred[256,1024]{0,1:T(8,128)(4,1)S(1)} %compare_and_fusion.2, bf16[256,1,8,128]{3,0,2,1:T(8,128)(2,1)S(1)} %get-tuple-element.452, bf16[8,1024,1,128]{3,1,2,0:T(8,128)(2,1)} %get-tuple-element.451, s32[]{:T(128)} %get-tuple-element.430), kind=kOutput, calls=%fused_computation.8.clone.1 | convolution fusion | flops 543160320 | bytes 9445888 | tf_op jit(solution)/shard_map/while/body/eval_jaxpr/tgjd,sgd->gjts/dot_general | solution.py:69
  259.2 5.2 %fusion.81 = f32[8,256]{1,0:T(8,128)S(1)} fusion(f32[1024,256,8]{1,0,2:T(8,128)} %get-tuple-element.380, f32[8,256]{1,0:T(8,128)S(1)} %select_maximum_fusion.2, pred[256,1024]{0,1:T(8,128)(4,1)S(1)} %compare_and_fusion.2), kind=kLoop, calls=%fused_computation.11.clone.1 | loop fusion | flops 8386560 | bytes 8667136 | tf_op jit(solution)/shard_map/while/body/eval_jaxpr/reduce_sum | solution.py:79
  265.2 3.4 fusion.83
  271.1 5.6 %fusion.80 = (f32[8,256]{1,0:T(8,128)S(1)}, f32[1024,256,8]{1,0,2:T(8,128)}) fusion(pred[256,1024]{0,1:T(8,128)(4,1)S(1)} %compare_and_fusion.2, bf16[256,1,8,128]{3,0,2,1:T(8,128)(2,1)S(1)} %get-tuple-element.452, bf16[8,1024,1,128]{3,1,2,0:T(8,128)(2,1)} %get-tuple-element.451, s32[]{:T(128)} %get-tuple-element.430), kind=kOutput, calls=%fused_computation.8.clone.1 | convolution fusion | flops 543160320 | bytes 9445888 | tf_op jit(solution)/shard_map/while/body/eval_jaxpr/tgjd,sgd->gjts/dot_general | solution.py:69
  276.7 5.3 %fusion.81 = f32[8,256]{1,0:T(8,128)S(1)} fusion(f32[1024,256,8]{1,0,2:T(8,128)} %get-tuple-element.380, f32[8,256]{1,0:T(8,128)S(1)} %select_maximum_fusion.2, pred[256,1024]{0,1:T(8,128)(4,1)S(1)} %compare_and_fusion.2), kind=kLoop, calls=%fused_computation.11.clone.1 | loop fusion | flops 8386560 | bytes 8667136 | tf_op jit(solution)/shard_map/while/body/eval_jaxpr/reduce_sum | solution.py:79
  282.6 3.4 fusion.83
  288.5 5.6 %fusion.80 = (f32[8,256]{1,0:T(8,128)S(1)}, f32[1024,256,8]{1,0,2:T(8,128)}) fusion(pred[256,1024]{0,1:T(8,128)(4,1)S(1)} %compare_and_fusion.2, bf16[256,1,8,128]{3,0,2,1:T(8,128)(2,1)S(1)} %get-tuple-element.452, bf16[8,1024,1,128]{3,1,2,0:T(8,128)(2,1)} %get-tuple-element.451, s32[]{:T(128)} %get-tuple-element.430), kind=kOutput, calls=%fused_computation.8.clone.1 | convolution fusion | flops 543160320 | bytes 9445888 | tf_op jit(solution)/shard_map/while/body/eval_jaxpr/tgjd,sgd->gjts/dot_general | solution.py:69
  294.1 5.2 %fusion.81 = f32[8,256]{1,0:T(8,128)S(1)} fusion(f32[1024,256,8]{1,0,2:T(8,128)} %get-tuple-element.380, f32[8,256]{1,0:T(8,128)S(1)} %select_maximum_fusion.2, pred[256,1024]{0,1:T(8,128)(4,1)S(1)} %compare_and_fusion.2), kind=kLoop, calls=%fused_computation.11.clone.1 | loop fusion | flops 8386560 | bytes 8667136 | tf_op jit(solution)/shard_map/while/body/eval_jaxpr/reduce_sum | solution.py:79
  299.9 3.4 fusion.83
  304.6 117.0 %while.10 = (s32[]{:T(128)}, f32[8,128,128]{2,1,0:T(8,128)S(1)}, f32[1]{0:T(128)}, s32[]{:T(128)}, f32[32,1]{0,1:T(1,128)S(1)}, /*index=5*/f32[32,8]{1,0:T(8,128...) while((s32[]{:T(128)}, f32[8,128,128]{2,1,0:T(8,128)S(1)}, ...), condition=%wide.region_1.2_spmd, body=%wide.region_0.1_spmd.sunk | while | flops 262161 | bytes 1573157 | solution.py:21
  306.5 1.2 bitcast_add_fusion.2
  310.3 1.2 bitcast_add_fusion.2
  314.1 1.2 bitcast_add_fusion.2
  317.8 1.2 bitcast_add_fusion.2
  321.6 1.2 bitcast_add_fusion.2
  325.4 1.2 bitcast_add_fusion.2
  329.2 1.2 bitcast_add_fusion.2
  332.9 1.2 bitcast_add_fusion.2
  336.7 1.2 bitcast_add_fusion.2
  340.5 1.2 bitcast_add_fusion.2
  344.3 1.2 bitcast_add_fusion.2
  348.0 1.2 bitcast_add_fusion.2
  351.8 1.2 bitcast_add_fusion.2
  355.6 1.2 bitcast_add_fusion.2
  359.4 1.2 bitcast_add_fusion.2
  363.1 1.2 bitcast_add_fusion.2
  366.9 1.2 bitcast_add_fusion.2
  370.7 1.2 bitcast_add_fusion.2
  374.5 1.2 bitcast_add_fusion.2
  378.2 1.2 bitcast_add_fusion.2
  382.0 1.2 bitcast_add_fusion.2
  385.8 1.2 bitcast_add_fusion.2
  393.3 1.2 bitcast_add_fusion.2
  397.1 1.2 bitcast_add_fusion.2
  416.0 1.2 bitcast_add_fusion.2
  419.8 1.2 bitcast_add_fusion.2
  422.3 2.8 fusion.30
  425.2 1.9 multiply_reduce_fusion
  427.4 13.4 %psum.7 = f32[256]{0:T(256)S(1)} all-reduce(f32[256]{0:T(256)S(1)} %get-tuple-element.262), channel_id=1, replica_groups=mesh['seq'=32,'heads'=8] {'heads'}, use_global_device_ids=true, to_apply=%region_3.4 | all-reduce | flops 256 | bytes 2048 | tf_op jit(solution)/shard_map/psum | solution.py:126
  (187 shorter events, 50.2 us)
Async XLA Ops:
  7.2 414.6 %copy-start = (bf16[256,1024]{1,0:T(8,128)(2,1)S(1)}, bf16[256,1024]{1,0:T(8,128)(2,1)}, u32[]{:S(2)}) copy-start(bf16[256,1024]{1,0:T(8,128)(2,1)} %param.13) | copy-start | bytes 1572868
  7.2 126.6 %all-gather.8.cloned.1.call-start = ((), (), s32[]{:S(2)}) async-start(), calls=%async_computation | async-start | bytes 2162688 | tf_op jit(solution)/shard_map/all_gather | solution.py:158
  7.9 155.6 %all-gather.10.cloned.1.call-start = ((), (), s32[]{:S(2)}) async-start(), calls=%async_computation.1 | async-start | bytes 2162688 | tf_op jit(solution)/shard_map/all_gather | solution.py:159
  8.7 295.9 %all-gather.12.cloned.1.call-start = ((), (), s32[]{:S(2)}) async-start(), calls=%async_computation.2 | async-start | bytes 17301504 | tf_op jit(solution)/shard_map/all_gather | solution.py:13
  171.5 5.8 %copy-start.1 = (f32[1024,256,8]{1,0,2:T(8,128)S(1)}, f32[1024,256,8]{1,0,2:T(8,128)}, u32[]{:S(2)}) copy-start(f32[1024,256,8]{1,0,2:T(8,128)} %get-tuple-element.380) | copy-start | bytes 25165828 | tf_op jit(solution)/shard_map/while
  188.8 6.0 %copy-start.1 = (f32[1024,256,8]{1,0,2:T(8,128)S(1)}, f32[1024,256,8]{1,0,2:T(8,128)}, u32[]{:S(2)}) copy-start(f32[1024,256,8]{1,0,2:T(8,128)} %get-tuple-element.380) | copy-start | bytes 25165828 | tf_op jit(solution)/shard_map/while
  206.3 5.8 %copy-start.1 = (f32[1024,256,8]{1,0,2:T(8,128)S(1)}, f32[1024,256,8]{1,0,2:T(8,128)}, u32[]{:S(2)}) copy-start(f32[1024,256,8]{1,0,2:T(8,128)} %get-tuple-element.380) | copy-start | bytes 25165828 | tf_op jit(solution)/shard_map/while
  223.9 5.9 %copy-start.1 = (f32[1024,256,8]{1,0,2:T(8,128)S(1)}, f32[1024,256,8]{1,0,2:T(8,128)}, u32[]{:S(2)}) copy-start(f32[1024,256,8]{1,0,2:T(8,128)} %get-tuple-element.380) | copy-start | bytes 25165828 | tf_op jit(solution)/shard_map/while
  241.4 6.3 %copy-start.1 = (f32[1024,256,8]{1,0,2:T(8,128)S(1)}, f32[1024,256,8]{1,0,2:T(8,128)}, u32[]{:S(2)}) copy-start(f32[1024,256,8]{1,0,2:T(8,128)} %get-tuple-element.380) | copy-start | bytes 25165828 | tf_op jit(solution)/shard_map/while
  259.2 6.0 %copy-start.1 = (f32[1024,256,8]{1,0,2:T(8,128)S(1)}, f32[1024,256,8]{1,0,2:T(8,128)}, u32[]{:S(2)}) copy-start(f32[1024,256,8]{1,0,2:T(8,128)} %get-tuple-element.380) | copy-start | bytes 25165828 | tf_op jit(solution)/shard_map/while
  276.7 5.9 %copy-start.1 = (f32[1024,256,8]{1,0,2:T(8,128)S(1)}, f32[1024,256,8]{1,0,2:T(8,128)}, u32[]{:S(2)}) copy-start(f32[1024,256,8]{1,0,2:T(8,128)} %get-tuple-element.380) | copy-start | bytes 25165828 | tf_op jit(solution)/shard_map/while
  294.1 5.8 %copy-start.1 = (f32[1024,256,8]{1,0,2:T(8,128)S(1)}, f32[1024,256,8]{1,0,2:T(8,128)}, u32[]{:S(2)}) copy-start(f32[1024,256,8]{1,0,2:T(8,128)} %get-tuple-element.380) | copy-start | bytes 25165828 | tf_op jit(solution)/shard_map/while
  303.4 118.3 %copy-start.2 = (s32[256]{0:T(256)S(1)}, s32[256]{0:T(256)}, u32[]{:S(2)}) copy-start(s32[256]{0:T(256)} %get-tuple-element.465) | copy-start | bytes 3076
  304.6 136.3 %copy-start.3 = (f32[1024]{0:T(1024)S(1)}, f32[1024]{0:T(1024)}, u32[]{:S(2)}) copy-start(f32[1024]{0:T(1024)} %param.17) | copy-start | bytes 12292
Sparse Core Ops, SparseCore 0:
  10.6 75.2 all-gather.7
  88.5 74.9 all-gather.9
  166.6 137.0 all-gather.11
where the time goes:
time: 452 us; the launch traced here: 448 us
  blocking collectives  126 us (28%)
  other arithmetic  93.2 us (21%)
  matrix products  80.3 us (18%)
  loops' own time  67.7 us (15%)
  local copies, waits for them, and re-layouts  34.4 us (8%)
  waiting for transfers between devices  31.1 us (7%)
  between operations  15.2 us (3%)
    unnamed x1, blocking collectives  69.7 us
    another operation x1, loops' own time, carried_in(): return lax.fori_loop(0, place, carried_one, state)  61.6 us
    dot_general x8, matrix products, block_update(): jnp.einsum('tgjd,sgd->gjts', queries, k_blk, preferred_element_type=jnp.f...  45.2 us
    all_gather x1, blocking collectives, body(): seg_keys = lax.all_gather(segment_ids, 'seq', axis=0, tiled=True)  43.2 us
    reduce_sum x8, other arithmetic, block_update(): den = den * corr + jnp.sum(p, axis=2)  42.1 us
    add x31, other arithmetic, combine_states(): factor[:, None, None] * state_e + state_l  36.9 us
    all_gather x1, waiting for transfers between devices, body(): values = lax.all_gather(soft_v, 'seq', axis=0, tiled=True)  29.7 us
    dot_general x8, matrix products, block_update(): jnp.einsum('gjts,sgd->gjtd', weights, v_blk, preferred_element_type=jnp.f...  27.6 us
  transfers between devices with their start and end apart: 3, of which 1 were waited for; matrix products, arithmetic and copies ran while one was open for 31% of the time, Pallas kernels for 0%

commit v1 on v0

--- a/solution.py
+++ b/solution.py
@@ -157,7 +157,19 @@
     carry = start_carry
     keys = lax.all_gather(soft_k, "seq", axis=0, tiled=True)
     values = lax.all_gather(soft_v, "seq", axis=0, tiled=True)
-    seg_keys = lax.all_gather(segment_ids, "seq", axis=0, tiled=True)
+
+    def manage_sheet(patch):
+        return jnp.concatenate(
+            jax.lax.all_to_all(
+                jnp.stack([patch] * jax.lax.axis_size("seq")),
+                axis_name="seq",
+                split_axis=0,
+                concat_axis=0,
+            ),
+            axis=0,
+        )
+
+    seg_keys = manage_sheet(segment_ids)
     length = keys.shape[0]
     rows = math.gcd(length, 1024)
     count_blk = length // rows

time: 452 us -> 452 us (level)
  blocking collectives: 126 us -> 83.8 us
  waiting for transfers between devices: 31.1 us -> 64.8 us
  starting transfers between devices: 0.11 us -> 8.58 us
    all_gather x1 -> x0, blocking collectives: 43.2 us -> none  [body(): seg_keys = lax.all_gather(segment_ids, 'seq', axis=0, tiled=True)]
    all_gather x1, waiting for transfers between devices: 29.7 us -> 63.4 us  [body(): values = lax.all_gather(soft_v, 'seq', axis=0, tiled=True)]
    all_to_all x0 -> x1, starting transfers between devices: none -> 8.47 us  [manage_sheet(): jax.lax.all_to_all(jnp.stack([patch] * jax.lax.axis_size('seq')), axis_na...]
  transfers between devices with their start and end apart: 3 -> 4, of which waited for: 1 -> 1; matrix products, arithmetic and copies ran while one was open for 31% -> 32% of each run, Pallas kernels for 0% -> 0%
where the time goes in v1:
time: 452 us; the launch traced here: 449 us
  other arithmetic  93.2 us (21%)
  blocking collectives  83.8 us (19%)
  matrix products  80.5 us (18%)
  loops' own time  67.4 us (15%)
  waiting for transfers between devices  64.8 us (14%)
  local copies, waits for them, and re-layouts  35 us (8%)
  between operations  15.3 us (3%)
  starting transfers between devices  8.58 us (2%)
    unnamed x1, blocking collectives  69.6 us
    all_gather x1, waiting for transfers between devices, body(): values = lax.all_gather(soft_v, 'seq', axis=0, tiled=True)  63.4 us
    another operation x1, loops' own time, carried_in(): return lax.fori_loop(0, place, carried_one, state)  61.6 us
    dot_general x8, matrix products, block_update(): jnp.einsum('tgjd,sgd->gjts', queries, k_blk, preferred_element_type=jnp.f...  45.5 us
    reduce_sum x8, other arithmetic, block_update(): den = den * corr + jnp.sum(p, axis=2)  42.2 us
    add x31, other arithmetic, combine_states(): factor[:, None, None] * state_e + state_l  36.9 us
    dot_general x8, matrix products, block_update(): jnp.einsum('gjts,sgd->gjtd', weights, v_blk, preferred_element_type=jnp.f...  27.6 us
    dynamic_slice x31, local copies, waits for them, and re-layouts, carried_one(): lax.dynamic_index_in_dim(a, step, 0, False)  18.1 us
  transfers between devices with their start and end apart: 4, of which 1 were waited for; matrix products, arithmetic and copies ran while one was open for 32% of the time, Pallas kernels for 0%

profile of v1, /device:TPU:230, one launch (start us, length us, event | category | flops | bytes accessed | tf_op | source)
XLA Modules:
  0.0 448.5 jit_solution(7864581760835617507)
XLA Ops:
  9.4 1.2 copy.50
  10.7 1.3 dynamic-slice.1
  12.6 1.2 fusion.61
  14.5 1.3 compare_convert_fusion.1
  16.6 2.1 convolution_add_fusion
  18.8 1.3 stack.2
  20.1 8.5 %all-to-all-start = ((s32[32,1,256]{2,1,0:T(1,128)}), s32[32,1,256]{2,1,0:T(1,128)S(1)}, u32[]{:S(2)}, u32[]{:S(2)}) async-start(s32[32,1,256]{2,1,0:T(1,128)} %stack.2), calls=%async_computation | async-start | bytes 65536 | tf_op jit(solution)/shard_map/all_to_all | solution.py:163
  28.6 69.6 %all-reduce.2 = (f32[32]{0:T(128)S(1)}, f32[256]{0:T(256)S(1)}) all-reduce(f32[32]{0:T(128)S(1)} %get-tuple-element.258, f32[256]{0:T(256)S(1)} %get-tuple-element.260), channel_id=2, replica_groups=mesh['seq'=32,'heads'=8] {'seq'}, use_global_device_ids=true, to_apply=%add | all-reduce | flops 288 | bytes 2304
  98.3 1.3 copy.44
  100.2 63.4 %all-gather.9.cloned.1.call-done = bf16[8192,128]{1,0:T(8,128)(2,1)} async-done(((bf16[256,128]{1,0:T(8,128)(2,1)}), bf16[8192,128]{1,0:T(8,128)(2,1)}) %all-gather.9.cloned.1.call-update) | async-done | bytes 2097168 | tf_op jit(solution)/shard_map/all_gather | solution.py:159
  163.7 139.1 %while.36 = (s32[]{:T(128)}, f32[8,256]{1,0:T(8,128)S(1)}, f32[8,256]{1,0:T(8,128)S(1)}, f32[8,256,128]{2,1,0:T(8,128)S(1)}, s32[8]{0:T(128)S(1)}, /*index=5*/s3...) while((s32[]{:T(128)}, f32[8,256]{1,0:T(8,128)S(1)}, ...), condition=%wide.region_7.8_spmd.clone, body=%wide.region_4.7_spmd.clone.sunk | while | flops 1098394880 | bytes 63070416 | solution.py:202
  166.0 5.6 %fusion.80 = (f32[8,256]{1,0:T(8,128)S(1)}, f32[1024,256,8]{1,0,2:T(8,128)}) fusion(pred[256,1024]{0,1:T(8,128)(4,1)S(1)} %compare_and_fusion.2, bf16[256,1,8,128]{3,0,2,1:T(8,128)(2,1)S(1)} %get-tuple-element.452, bf16[8,1024,1,128]{3,1,2,0:T(8,128)(2,1)} %get-tuple-element.451, s32[]{:T(128)} %get-tuple-element.430), kind=kOutput, calls=%fused_computation.8.clone.1 | convolution fusion | flops 543160320 | bytes 9445888 | tf_op jit(solution)/shard_map/while/body/eval_jaxpr/tgjd,sgd->gjts/dot_general | solution.py:69
  171.6 5.2 %fusion.81 = f32[8,256]{1,0:T(8,128)S(1)} fusion(f32[1024,256,8]{1,0,2:T(8,128)} %get-tuple-element.380, f32[8,256]{1,0:T(8,128)S(1)} %select_maximum_fusion.2, pred[256,1024]{0,1:T(8,128)(4,1)S(1)} %compare_and_fusion.2), kind=kLoop, calls=%fused_computation.11.clone.1 | loop fusion | flops 8386560 | bytes 8667136 | tf_op jit(solution)/shard_map/while/body/eval_jaxpr/reduce_sum | solution.py:79
  177.3 3.4 fusion.83
  183.1 5.6 %fusion.80 = (f32[8,256]{1,0:T(8,128)S(1)}, f32[1024,256,8]{1,0,2:T(8,128)}) fusion(pred[256,1024]{0,1:T(8,128)(4,1)S(1)} %compare_and_fusion.2, bf16[256,1,8,128]{3,0,2,1:T(8,128)(2,1)S(1)} %get-tuple-element.452, bf16[8,1024,1,128]{3,1,2,0:T(8,128)(2,1)} %get-tuple-element.451, s32[]{:T(128)} %get-tuple-element.430), kind=kOutput, calls=%fused_computation.8.clone.1 | convolution fusion | flops 543160320 | bytes 9445888 | tf_op jit(solution)/shard_map/while/body/eval_jaxpr/tgjd,sgd->gjts/dot_general | solution.py:69
  188.7 5.3 %fusion.81 = f32[8,256]{1,0:T(8,128)S(1)} fusion(f32[1024,256,8]{1,0,2:T(8,128)} %get-tuple-element.380, f32[8,256]{1,0:T(8,128)S(1)} %select_maximum_fusion.2, pred[256,1024]{0,1:T(8,128)(4,1)S(1)} %compare_and_fusion.2), kind=kLoop, calls=%fused_computation.11.clone.1 | loop fusion | flops 8386560 | bytes 8667136 | tf_op jit(solution)/shard_map/while/body/eval_jaxpr/reduce_sum | solution.py:79
  194.7 3.4 fusion.83
  200.5 5.6 %fusion.80 = (f32[8,256]{1,0:T(8,128)S(1)}, f32[1024,256,8]{1,0,2:T(8,128)}) fusion(pred[256,1024]{0,1:T(8,128)(4,1)S(1)} %compare_and_fusion.2, bf16[256,1,8,128]{3,0,2,1:T(8,128)(2,1)S(1)} %get-tuple-element.452, bf16[8,1024,1,128]{3,1,2,0:T(8,128)(2,1)} %get-tuple-element.451, s32[]{:T(128)} %get-tuple-element.430), kind=kOutput, calls=%fused_computation.8.clone.1 | convolution fusion | flops 543160320 | bytes 9445888 | tf_op jit(solution)/shard_map/while/body/eval_jaxpr/tgjd,sgd->gjts/dot_general | solution.py:69
  206.1 5.2 %fusion.81 = f32[8,256]{1,0:T(8,128)S(1)} fusion(f32[1024,256,8]{1,0,2:T(8,128)} %get-tuple-element.380, f32[8,256]{1,0:T(8,128)S(1)} %select_maximum_fusion.2, pred[256,1024]{0,1:T(8,128)(4,1)S(1)} %compare_and_fusion.2), kind=kLoop, calls=%fused_computation.11.clone.1 | loop fusion | flops 8386560 | bytes 8667136 | tf_op jit(solution)/shard_map/while/body/eval_jaxpr/reduce_sum | solution.py:79
  211.9 3.4 fusion.83
  217.6 6.2 %fusion.80 = (f32[8,256]{1,0:T(8,128)S(1)}, f32[1024,256,8]{1,0,2:T(8,128)}) fusion(pred[256,1024]{0,1:T(8,128)(4,1)S(1)} %compare_and_fusion.2, bf16[256,1,8,128]{3,0,2,1:T(8,128)(2,1)S(1)} %get-tuple-element.452, bf16[8,1024,1,128]{3,1,2,0:T(8,128)(2,1)} %get-tuple-element.451, s32[]{:T(128)} %get-tuple-element.430), kind=kOutput, calls=%fused_computation.8.clone.1 | convolution fusion | flops 543160320 | bytes 9445888 | tf_op jit(solution)/shard_map/while/body/eval_jaxpr/tgjd,sgd->gjts/dot_general | solution.py:69
  223.9 5.3 %fusion.81 = f32[8,256]{1,0:T(8,128)S(1)} fusion(f32[1024,256,8]{1,0,2:T(8,128)} %get-tuple-element.380, f32[8,256]{1,0:T(8,128)S(1)} %select_maximum_fusion.2, pred[256,1024]{0,1:T(8,128)(4,1)S(1)} %compare_and_fusion.2), kind=kLoop, calls=%fused_computation.11.clone.1 | loop fusion | flops 8386560 | bytes 8667136 | tf_op jit(solution)/shard_map/while/body/eval_jaxpr/reduce_sum | solution.py:79
  229.8 3.5 fusion.83
  235.6 5.6 %fusion.80 = (f32[8,256]{1,0:T(8,128)S(1)}, f32[1024,256,8]{1,0,2:T(8,128)}) fusion(pred[256,1024]{0,1:T(8,128)(4,1)S(1)} %compare_and_fusion.2, bf16[256,1,8,128]{3,0,2,1:T(8,128)(2,1)S(1)} %get-tuple-element.452, bf16[8,1024,1,128]{3,1,2,0:T(8,128)(2,1)} %get-tuple-element.451, s32[]{:T(128)} %get-tuple-element.430), kind=kOutput, calls=%fused_computation.8.clone.1 | convolution fusion | flops 543160320 | bytes 9445888 | tf_op jit(solution)/shard_map/while/body/eval_jaxpr/tgjd,sgd->gjts/dot_general | solution.py:69
  241.2 5.3 %fusion.81 = f32[8,256]{1,0:T(8,128)S(1)} fusion(f32[1024,256,8]{1,0,2:T(8,128)} %get-tuple-element.380, f32[8,256]{1,0:T(8,128)S(1)} %select_maximum_fusion.2, pred[256,1024]{0,1:T(8,128)(4,1)S(1)} %compare_and_fusion.2), kind=kLoop, calls=%fused_computation.11.clone.1 | loop fusion | flops 8386560 | bytes 8667136 | tf_op jit(solution)/shard_map/while/body/eval_jaxpr/reduce_sum | solution.py:79
  247.4 3.4 fusion.83
  253.2 5.6 %fusion.80 = (f32[8,256]{1,0:T(8,128)S(1)}, f32[1024,256,8]{1,0,2:T(8,128)}) fusion(pred[256,1024]{0,1:T(8,128)(4,1)S(1)} %compare_and_fusion.2, bf16[256,1,8,128]{3,0,2,1:T(8,128)(2,1)S(1)} %get-tuple-element.452, bf16[8,1024,1,128]{3,1,2,0:T(8,128)(2,1)} %get-tuple-element.451, s32[]{:T(128)} %get-tuple-element.430), kind=kOutput, calls=%fused_computation.8.clone.1 | convolution fusion | flops 543160320 | bytes 9445888 | tf_op jit(solution)/shard_map/while/body/eval_jaxpr/tgjd,sgd->gjts/dot_general | solution.py:69
  258.8 5.2 %fusion.81 = f32[8,256]{1,0:T(8,128)S(1)} fusion(f32[1024,256,8]{1,0,2:T(8,128)} %get-tuple-element.380, f32[8,256]{1,0:T(8,128)S(1)} %select_maximum_fusion.2, pred[256,1024]{0,1:T(8,128)(4,1)S(1)} %compare_and_fusion.2), kind=kLoop, calls=%fused_computation.11.clone.1 | loop fusion | flops 8386560 | bytes 8667136 | tf_op jit(solution)/shard_map/while/body/eval_jaxpr/reduce_sum | solution.py:79
  264.8 3.4 fusion.83
  270.6 5.6 %fusion.80 = (f32[8,256]{1,0:T(8,128)S(1)}, f32[1024,256,8]{1,0,2:T(8,128)}) fusion(pred[256,1024]{0,1:T(8,128)(4,1)S(1)} %compare_and_fusion.2, bf16[256,1,8,128]{3,0,2,1:T(8,128)(2,1)S(1)} %get-tuple-element.452, bf16[8,1024,1,128]{3,1,2,0:T(8,128)(2,1)} %get-tuple-element.451, s32[]{:T(128)} %get-tuple-element.430), kind=kOutput, calls=%fused_computation.8.clone.1 | convolution fusion | flops 543160320 | bytes 9445888 | tf_op jit(solution)/shard_map/while/body/eval_jaxpr/tgjd,sgd->gjts/dot_general | solution.py:69
  276.2 5.3 %fusion.81 = f32[8,256]{1,0:T(8,128)S(1)} fusion(f32[1024,256,8]{1,0,2:T(8,128)} %get-tuple-element.380, f32[8,256]{1,0:T(8,128)S(1)} %select_maximum_fusion.2, pred[256,1024]{0,1:T(8,128)(4,1)S(1)} %compare_and_fusion.2), kind=kLoop, calls=%fused_computation.11.clone.1 | loop fusion | flops 8386560 | bytes 8667136 | tf_op jit(solution)/shard_map/while/body/eval_jaxpr/reduce_sum | solution.py:79
  282.1 3.4 fusion.83
  287.9 5.6 %fusion.80 = (f32[8,256]{1,0:T(8,128)S(1)}, f32[1024,256,8]{1,0,2:T(8,128)}) fusion(pred[256,1024]{0,1:T(8,128)(4,1)S(1)} %compare_and_fusion.2, bf16[256,1,8,128]{3,0,2,1:T(8,128)(2,1)S(1)} %get-tuple-element.452, bf16[8,1024,1,128]{3,1,2,0:T(8,128)(2,1)} %get-tuple-element.451, s32[]{:T(128)} %get-tuple-element.430), kind=kOutput, calls=%fused_computation.8.clone.1 | convolution fusion | flops 543160320 | bytes 9445888 | tf_op jit(solution)/shard_map/while/body/eval_jaxpr/tgjd,sgd->gjts/dot_general | solution.py:69
  293.5 5.2 %fusion.81 = f32[8,256]{1,0:T(8,128)S(1)} fusion(f32[1024,256,8]{1,0,2:T(8,128)} %get-tuple-element.380, f32[8,256]{1,0:T(8,128)S(1)} %select_maximum_fusion.2, pred[256,1024]{0,1:T(8,128)(4,1)S(1)} %compare_and_fusion.2), kind=kLoop, calls=%fused_computation.11.clone.1 | loop fusion | flops 8386560 | bytes 8667136 | tf_op jit(solution)/shard_map/while/body/eval_jaxpr/reduce_sum | solution.py:79
  299.3 3.4 fusion.83
  304.0 117.0 %while.10 = (s32[]{:T(128)}, f32[8,128,128]{2,1,0:T(8,128)S(1)}, f32[1]{0:T(128)}, s32[]{:T(128)}, f32[32,1]{0,1:T(1,128)S(1)}, /*index=5*/f32[32,8]{1,0:T(8,128...) while((s32[]{:T(128)}, f32[8,128,128]{2,1,0:T(8,128)S(1)}, ...), condition=%wide.region_1.2_spmd, body=%wide.region_0.1_spmd.sunk | while | flops 262161 | bytes 1573157 | solution.py:21
  305.9 1.2 bitcast_add_fusion.2
  309.7 1.2 bitcast_add_fusion.2
  313.5 1.2 bitcast_add_fusion.2
  317.2 1.2 bitcast_add_fusion.2
  321.0 1.2 bitcast_add_fusion.2
  324.8 1.2 bitcast_add_fusion.2
  328.6 1.2 bitcast_add_fusion.2
  332.3 1.2 bitcast_add_fusion.2
  336.1 1.2 bitcast_add_fusion.2
  339.9 1.2 bitcast_add_fusion.2
  343.7 1.2 bitcast_add_fusion.2
  347.4 1.2 bitcast_add_fusion.2
  351.2 1.2 bitcast_add_fusion.2
  355.0 1.2 bitcast_add_fusion.2
  358.8 1.2 bitcast_add_fusion.2
  362.5 1.2 bitcast_add_fusion.2
  366.3 1.2 bitcast_add_fusion.2
  370.1 1.2 bitcast_add_fusion.2
  373.9 1.2 bitcast_add_fusion.2
  377.6 1.2 bitcast_add_fusion.2
  381.4 1.2 bitcast_add_fusion.2
  385.2 1.2 bitcast_add_fusion.2
  389.0 1.2 bitcast_add_fusion.2
  404.1 1.2 bitcast_add_fusion.2
  407.9 1.2 bitcast_add_fusion.2
  421.7 2.8 fusion.30
  424.6 1.9 multiply_reduce_fusion
  426.8 14.2 %psum.7 = f32[256]{0:T(256)S(1)} all-reduce(f32[256]{0:T(256)S(1)} %get-tuple-element.262), channel_id=1, replica_groups=mesh['seq'=32,'heads'=8] {'heads'}, use_global_device_ids=true, to_apply=%region_3.4 | all-reduce | flops 256 | bytes 2048 | tf_op jit(solution)/shard_map/psum | solution.py:126
  (189 shorter events, 50.7 us)
Async XLA Ops:
  7.2 414.0 %copy-start = (bf16[256,1024]{1,0:T(8,128)(2,1)S(1)}, bf16[256,1024]{1,0:T(8,128)(2,1)}, u32[]{:S(2)}) copy-start(bf16[256,1024]{1,0:T(8,128)(2,1)} %param.13) | copy-start | bytes 1572868
  7.2 93.1 %all-gather.7.cloned.1.call-start = ((), (), s32[]{:S(2)}) async-start(), calls=%async_computation.1 | async-start | bytes 2162688 | tf_op jit(solution)/shard_map/all_gather | solution.py:158
  7.9 155.7 %all-gather.9.cloned.1.call-start = ((), (), s32[]{:S(2)}) async-start(), calls=%async_computation.2 | async-start | bytes 2162688 | tf_op jit(solution)/shard_map/all_gather | solution.py:159
  8.7 295.3 %all-gather.11.cloned.1.call-start = ((), (), s32[]{:S(2)}) async-start(), calls=%async_computation.3 | async-start | bytes 17301504 | tf_op jit(solution)/shard_map/all_gather | solution.py:13
  20.1 80.0 %all-to-all-start = ((s32[32,1,256]{2,1,0:T(1,128)}), s32[32,1,256]{2,1,0:T(1,128)S(1)}, u32[]{:S(2)}, u32[]{:S(2)}) async-start(s32[32,1,256]{2,1,0:T(1,128)} %stack.2), calls=%async_computation | async-start | bytes 65536 | tf_op jit(solution)/shard_map/all_to_all | solution.py:163
  171.6 5.8 %copy-start.1 = (f32[1024,256,8]{1,0,2:T(8,128)S(1)}, f32[1024,256,8]{1,0,2:T(8,128)}, u32[]{:S(2)}) copy-start(f32[1024,256,8]{1,0,2:T(8,128)} %get-tuple-element.380) | copy-start | bytes 25165828 | tf_op jit(solution)/shard_map/while
  188.7 6.0 %copy-start.1 = (f32[1024,256,8]{1,0,2:T(8,128)S(1)}, f32[1024,256,8]{1,0,2:T(8,128)}, u32[]{:S(2)}) copy-start(f32[1024,256,8]{1,0,2:T(8,128)} %get-tuple-element.380) | copy-start | bytes 25165828 | tf_op jit(solution)/shard_map/while
  206.1 5.8 %copy-start.1 = (f32[1024,256,8]{1,0,2:T(8,128)S(1)}, f32[1024,256,8]{1,0,2:T(8,128)}, u32[]{:S(2)}) copy-start(f32[1024,256,8]{1,0,2:T(8,128)} %get-tuple-element.380) | copy-start | bytes 25165828 | tf_op jit(solution)/shard_map/while
  223.9 5.9 %copy-start.1 = (f32[1024,256,8]{1,0,2:T(8,128)S(1)}, f32[1024,256,8]{1,0,2:T(8,128)}, u32[]{:S(2)}) copy-start(f32[1024,256,8]{1,0,2:T(8,128)} %get-tuple-element.380) | copy-start | bytes 25165828 | tf_op jit(solution)/shard_map/while
  241.2 6.2 %copy-start.1 = (f32[1024,256,8]{1,0,2:T(8,128)S(1)}, f32[1024,256,8]{1,0,2:T(8,128)}, u32[]{:S(2)}) copy-start(f32[1024,256,8]{1,0,2:T(8,128)} %get-tuple-element.380) | copy-start | bytes 25165828 | tf_op jit(solution)/shard_map/while
  258.8 6.0 %copy-start.1 = (f32[1024,256,8]{1,0,2:T(8,128)S(1)}, f32[1024,256,8]{1,0,2:T(8,128)}, u32[]{:S(2)}) copy-start(f32[1024,256,8]{1,0,2:T(8,128)} %get-tuple-element.380) | copy-start | bytes 25165828 | tf_op jit(solution)/shard_map/while
  276.2 5.9 %copy-start.1 = (f32[1024,256,8]{1,0,2:T(8,128)S(1)}, f32[1024,256,8]{1,0,2:T(8,128)}, u32[]{:S(2)}) copy-start(f32[1024,256,8]{1,0,2:T(8,128)} %get-tuple-element.380) | copy-start | bytes 25165828 | tf_op jit(solution)/shard_map/while
  293.5 5.8 %copy-start.1 = (f32[1024,256,8]{1,0,2:T(8,128)S(1)}, f32[1024,256,8]{1,0,2:T(8,128)}, u32[]{:S(2)}) copy-start(f32[1024,256,8]{1,0,2:T(8,128)} %get-tuple-element.380) | copy-start | bytes 25165828 | tf_op jit(solution)/shard_map/while
  302.8 118.3 %copy-start.2 = (s32[256]{0:T(256)S(1)}, s32[256]{0:T(256)}, u32[]{:S(2)}) copy-start(s32[256]{0:T(256)} %get-tuple-element.466) | copy-start | bytes 3076
  304.0 137.1 %copy-start.3 = (f32[1024]{0:T(1024)S(1)}, f32[1024]{0:T(1024)}, u32[]{:S(2)}) copy-start(f32[1024]{0:T(1024)} %param.17) | copy-start | bytes 12292
Sparse Core Ops, SparseCore 0:
  10.6 75.4 all-gather.6
  88.7 74.9 all-gather.8
  166.8 137.0 all-gather.10
